TPU v7x, 512 devices: a whole 4x4x16 slice. The times are simulated.
512 devices in a mesh: line: 16 (over z), bus: 32 (over x, y, core).
Axes of the slice: x: 4, y: 4, z: 16, core: 2. Of those that a mesh axis runs over, the one named last changes fastest.
Arguments:
- transfer_factors: float32 [4096, 65536], P('line', 'bus'), may hold values from -0.24 to 0.24
- line_flows: float32 [4096], P('line'), may hold values from -6 to 6
- from_bus: int32 [4096], replicated, may hold values from 0 to 65535
- to_bus: int32 [4096], replicated, may hold values from 0 to 65535
- tripped: int32 [2, 64], replicated, may hold values from 0 to 4095, as said below
Outputs:
- new_factors: float32 [4096, 65536], P('line', 'bus')
- new_flows: float32 [4096], P('line')
Inputs may be any that keep to these rules, and one draw needn't show every extreme that they name: No line is tripped twice; in every segment at most 8 tripped lines lie in one aligned block of 256 consecutive lines, and some block holds exactly 8.
All inputs are finite; a program needn't handle non-finite values.
Results may differ from a plain program's by a relative error of at most 0.00018.
Values sent between devices are 32-bit elements; how exact they have to be, the bound alone decides.
A program may use at most 64 MiB of HBM per device.

v0:
```python
import jax
import jax.numpy as jnp
from jax import lax
from jax.sharding import PartitionSpec as P


def chol_solve(factor_lower, right):
    middle = lax.linalg.triangular_solve(factor_lower, right, left_side=True, lower=True)
    return lax.linalg.triangular_solve(
        factor_lower, middle, left_side=True, lower=True, transpose_a=True
    )


def column_select(col_global, from_bus, to_bus, outage_ids):
    from_ids = jnp.take(from_bus, outage_ids)
    to_ids = jnp.take(to_bus, outage_ids)
    return (col_global[:, None] == from_ids[None, :]).astype(jnp.float32) - (
        col_global[:, None] == to_ids[None, :]
    ).astype(jnp.float32)


def per_device(transfer_factors, line_flows, from_bus, to_bus, tripped):
    precise = lax.Precision.HIGHEST
    local_rows, local_cols = transfer_factors.shape
    outages = tripped.shape[1]
    line_index = lax.axis_index("line")
    bus_index = lax.axis_index("bus")
    row_global = line_index * local_rows + jnp.arange(local_rows, dtype=jnp.int32)
    col_global = bus_index * local_cols + jnp.arange(local_cols, dtype=jnp.int32)
    factors = transfer_factors
    flows_now = line_flows
    identity = jnp.eye(outages, dtype=jnp.float32)
    for segment_index in range(tripped.shape[0]):
        outage_ids = tripped[segment_index]
        terminal_select = column_select(col_global, from_bus, to_bus, outage_ids)
        outage_select = (outage_ids[:, None] == row_global[None, :]).astype(jnp.float32)
        terminal_part = jnp.dot(factors, terminal_select, precision=precise)
        terminal = lax.psum(terminal_part, "bus")
        outage_terms = lax.psum(jnp.dot(outage_select, terminal, precision=precise), "line")
        outage_rows, outage_flows = lax.psum(
            (
                jnp.dot(outage_select, factors, precision=precise),
                jnp.dot(outage_select, flows_now, precision=precise),
            ),
            "line",
        )
        capacitance = identity - outage_terms
        factor_lower = jnp.linalg.cholesky(jnp.dot(capacitance, capacitance.T, precision=precise))
        update_weights = chol_solve(
            factor_lower, jnp.dot(capacitance, terminal.T, precision=precise)
        )
        factors = factors + jnp.dot(update_weights.T, outage_rows, precision=precise)
        flows_now = flows_now + jnp.dot(update_weights.T, outage_flows, precision=precise)
        keep_mask = 1.0 - jnp.sum(outage_select, axis=0)
        factors = factors * keep_mask[:, None]
        flows_now = flows_now * keep_mask
    return (factors, flows_now)


def solution(mesh):
    placed = (P("line", "bus"), P("line"), P(), P(), P())
    return jax.shard_map(
        per_device,
        mesh=mesh,
        in_specs=placed,
        out_specs=(P("line", "bus"), P("line")),
        check_vma=False,
    )
```

profile of v0, /device:TPU:2, one launch (start us, length us, event | category | flops | bytes accessed | tf_op | source)
XLA Modules:
  0.0 564.4 jit_solution(1560953369744594784)
XLA Ops:
  7.2 0.0 all-reduce.7.cloned.1.call-start
  7.3 0.8 compare_select_fusion
  8.1 0.8 gather_fusion.1
  8.9 1.5 gather_fusion
  10.4 4.6 convolution_bitcast_fusion
  15.0 0.0 all-reduce.7.cloned.1.call-update
  15.0 0.0 all-reduce.9.cloned.1.call-start
  15.1 1.7 fusion.25
  16.9 0.0 all-reduce.11.cloned.1.call-start
  16.9 0.8 gather_fusion.3
  17.7 0.8 gather_fusion.2
  18.5 0.2 convolution_bitcast_fusion.2
  18.6 0.1 fusion.30
  18.8 126.4 %all-reduce.7.cloned.1.call-done = f32[256,64]{0,1:T(8,128)} async-done(((f32[256,64]{0,1:T(8,128)}), f32[256,64]{0,1:T(8,128)}) %all-reduce.7.cloned.1.call-update) | async-done | bytes 65552 | tf_op jit(solution)/shard_map/psum | solution.py:38
  145.2 1.1 fusion.27
  146.3 57.0 %all-reduce.1 = (f32[64,64]{1,0:T(8,128)S(1)}, f32[64]{0:T(128)S(1)}) all-reduce(f32[64,64]{1,0:T(8,128)S(1)} %fusion.27, f32[64]{0:T(128)S(1)} %convolution_bitcast_fusion.2), channel_id=1, replica_groups=mesh['line'=16,'bus'=32] {'line'}, use_global_device_ids=true, to_apply=%region_1.3 | all-reduce | flops 4160 | bytes 33280 | tf_op jit(solution)/shard_map/psum | solution.py:39
  203.2 0.2 fusion.60
  203.4 0.1 copy.11
  203.5 5.8 %cholesky.44 = f32[64,64]{1,0:T(8,128)S(1)} custom-call(f32[64,64]{1,0:T(8,128)S(1)} %fusion.46), custom_call_target="Cholesky" | custom-call | tf_op jit(solution)/shard_map/jit(cholesky)/cholesky | solution.py:48
  209.4 0.6 compare_reduce_fusion.1
  210.0 0.7 fusion.35
  210.7 4.9 custom-call.11
  215.6 1.1 fusion.59
  216.7 0.3 fusion.42
  216.9 0.2 fusion.44
  217.1 0.1 fusion.33
  217.3 0.2 convolution_bitcast_fusion.1
  217.5 67.4 %all-reduce.9.cloned.1.call-done = f32[64,2048]{1,0:T(8,128)} async-done(((f32[64,2048]{1,0:T(8,128)}), f32[64,2048]{1,0:T(8,128)}) %all-reduce.9.cloned.1.call-update) | async-done | bytes 524304 | tf_op jit(solution)/shard_map/psum | solution.py:40
  284.8 3.7 fusion.1
  288.5 3.0 fusion.2
  291.5 0.0 all-reduce.13.cloned.1.call-start
  291.5 1.7 fusion.20
  293.3 120.7 %all-reduce.11.cloned.1.call-done = f32[256,64]{0,1:T(8,128)} async-done(((f32[256,64]{0,1:T(8,128)}), f32[256,64]{0,1:T(8,128)}) %all-reduce.11.cloned.1.call-update) | async-done | bytes 65552 | tf_op jit(solution)/shard_map/psum | solution.py:38
  414.0 1.1 fusion.22
  415.1 56.9 %all-reduce = (f32[64,64]{1,0:T(8,128)S(1)}, f32[64]{0:T(128)S(1)}) all-reduce(f32[64,64]{1,0:T(8,128)S(1)} %fusion.22, f32[64]{0:T(128)S(1)} %convolution_bitcast_fusion.1), channel_id=1, replica_groups=mesh['line'=16,'bus'=32] {'line'}, use_global_device_ids=true, to_apply=%region_7.12 | all-reduce | flops 4160 | bytes 33280 | tf_op jit(solution)/shard_map/psum | solution.py:39
  472.0 0.2 fusion.62
  472.2 0.1 copy.12
  472.3 5.8 %cholesky.55 = f32[64,64]{1,0:T(8,128)S(1)} custom-call(f32[64,64]{1,0:T(8,128)S(1)} %fusion.41), custom_call_target="Cholesky" | custom-call | tf_op jit(solution)/shard_map/jit(cholesky)/cholesky | solution.py:48
  478.1 0.6 compare_reduce_fusion
  478.8 0.7 fusion.36
  479.5 4.9 custom-call.13
  484.3 1.1 fusion.61
  485.4 0.3 fusion.37
  485.7 0.2 fusion.39
  485.9 0.1 fusion.31
  486.0 0.6 add_multiply_fusion
  486.6 67.0 %all-reduce.13.cloned.1.call-done = f32[64,2048]{1,0:T(8,128)} async-done(((f32[64,2048]{1,0:T(8,128)}), f32[64,2048]{1,0:T(8,128)}) %all-reduce.13.cloned.1.call-update) | async-done | bytes 524304 | tf_op jit(solution)/shard_map/psum | solution.py:40
  553.6 4.3 fusion
  (24 shorter events, 0.2 us)
Async XLA Ops:
  7.2 0.9 copy-start
  7.2 7.9 %copy-start.3 = (s32[2,64]{1,0:T(2,128)S(1)}, s32[2,64]{1,0:T(2,128)}, u32[]{:S(2)}) copy-start(s32[2,64]{1,0:T(2,128)} %param.16) | copy-start | bytes 1540
  7.2 7.9 %copy-start.2 = (f32[256,2048]{1,0:T(8,128)S(1)}, f32[256,2048]{1,0:T(8,128)}, u32[]{:S(2)}) copy-start(f32[256,2048]{1,0:T(8,128)} %param.12) | copy-start | bytes 6291460
  7.2 138.0 %all-reduce.7.cloned.1.call-start = ((), (), s32[]{:S(2)}) async-start(), calls=%async_computation | async-start | bytes 131072 | tf_op jit(solution)/shard_map/psum | solution.py:38
  15.0 2.7 copy-start.1
  15.0 269.8 %all-reduce.9.cloned.1.call-start = ((), (), s32[]{:S(2)}) async-start(), calls=%async_computation.1 | async-start | bytes 1048576 | tf_op jit(solution)/shard_map/psum | solution.py:40
  15.1 3.4 copy-start.4
  16.9 397.1 %all-reduce.11.cloned.1.call-start = ((), (), s32[]{:S(2)}) async-start(), calls=%async_computation.2 | async-start | bytes 131072 | tf_op jit(solution)/shard_map/psum | solution.py:38
  291.5 262.2 %all-reduce.13.cloned.1.call-start = ((), (), s32[]{:S(2)}) async-start(), calls=%async_computation.3 | async-start | bytes 1048576 | tf_op jit(solution)/shard_map/psum | solution.py:40
Sparse Core Ops, SparseCore 0:
  15.1 130.0 all-reduce.6
  148.2 136.5 all-reduce.8
  291.6 122.3 all-reduce.10
  416.8 136.7 all-reduce.12
where the time goes:
time: 565 us; the launch traced here: 564 us
  waiting for transfers between devices  382 us (68%)
  blocking collectives  114 us (20%)
  other arithmetic  25.7 us (5%)
  matrix products  25.1 us (4%)
  between operations  14 us (2%)
    psum x2, waiting for transfers between devices, per_device(): terminal = lax.psum(terminal_part, 'bus')  247 us
    psum x2, waiting for transfers between devices, per_device(): lax.psum((jnp.dot(outage_select, factors, precision=precise), jnp.dot(out...  134 us
    psum x2, blocking collectives, per_device(): lax.psum(jnp.dot(outage_select, terminal, precision=precise), 'line')  114 us
    another operation x6, other arithmetic, per_device(): jnp.linalg.cholesky(jnp.dot(capacitance, capacitance.T, precision=precise))  13 us
  transfers between devices with their start and end apart: 4, of which 4 were waited for; matrix products, arithmetic and copies ran while one was open for 6% of the time, Pallas kernels for 0%

commit v1 on v0

--- a/solution.py
+++ b/solution.py
@@ -1,7 +1,16 @@
+import functools
 import jax
 import jax.numpy as jnp
 from jax import lax
 from jax.sharding import PartitionSpec as P
+
+
+def report_thing(obj, lane_axis):
+    piece_now = lax.all_gather(obj, axis_name=lane_axis)
+    return jnp.sum(piece_now, axis=0)
+
+
+sector_number = functools.partial(report_thing, lane_axis="bus")
 
 
 def chol_solve(factor_lower, right):
@@ -35,7 +44,7 @@
         terminal_select = column_select(col_global, from_bus, to_bus, outage_ids)
         outage_select = (outage_ids[:, None] == row_global[None, :]).astype(jnp.float32)
         terminal_part = jnp.dot(factors, terminal_select, precision=precise)
-        terminal = lax.psum(terminal_part, "bus")
+        terminal = sector_number(terminal_part)
         outage_terms = lax.psum(jnp.dot(outage_select, terminal, precision=precise), "line")
         outage_rows, outage_flows = lax.psum(
             (

time: 565 us -> 317 us (0.56)
  waiting for transfers between devices: 382 us -> 130 us
    psum x2 -> x0, waiting for transfers between devices: 247 us -> none  [per_device(): terminal = lax.psum(terminal_part, 'bus')]
    psum x2, waiting for transfers between devices: 134 us -> 14.5 us  [per_device(): lax.psum((jnp.dot(outage_select, factors, precision=precise), jnp.dot(out...]
    all_gather x0 -> x2, waiting for transfers between devices: none -> 115 us  [report_thing(): piece_now = lax.all_gather(obj, axis_name=lane_axis)]
  transfers between devices with their start and end apart: 4 -> 4, of which waited for: 4 -> 4; matrix products, arithmetic and copies ran while one was open for 6% -> 12% of each run, Pallas kernels for 0% -> 0%
where the time goes in v1:
time: 317 us; the launch traced here: 316 us
  waiting for transfers between devices  130 us (41%)
  blocking collectives  114 us (36%)
  other arithmetic  26.2 us (8%)
  matrix products  21.8 us (7%)
  between operations  15.8 us (5%)
  local copies, waits for them, and re-layouts  8.44 us (3%)
    all_gather x2, waiting for transfers between devices, report_thing(): piece_now = lax.all_gather(obj, axis_name=lane_axis)  115 us
    psum x2, blocking collectives, per_device(): lax.psum(jnp.dot(outage_select, terminal, precision=precise), 'line')  114 us
    psum x2, waiting for transfers between devices, per_device(): lax.psum((jnp.dot(outage_select, factors, precision=precise), jnp.dot(out...  14.5 us
    another operation x6, other arithmetic, per_device(): jnp.linalg.cholesky(jnp.dot(capacitance, capacitance.T, precision=precise))  13 us
    another operation x4, other arithmetic, chol_solve(): lax.linalg.triangular_solve(factor_lower, middle, left_side=True, lower=T...  11.1 us
    dot_general x2, matrix products, per_device(): jnp.dot(update_weights.T, outage_rows, precision=precise)  7.94 us
    dot_general x2, matrix products, per_device(): terminal_part = jnp.dot(factors, terminal_select, precision=precise)  7.51 us
  transfers between devices with their start and end apart: 4, of which 4 were waited for; matrix products, arithmetic and copies ran while one was open for 12% of the time, Pallas kernels for 0%

profile of v1, /device:TPU:2, one launch (start us, length us, event | category | flops | bytes accessed | tf_op | source)
XLA Modules:
  0.0 316.3 jit_solution(18395131054375255070)
XLA Ops:
  8.1 0.8 compare_select_fusion
  8.9 0.8 gather_fusion
  9.7 1.5 gather_fusion.1
  11.2 4.6 %convolution_bitcast_fusion = f32[256,64]{0,1:T(8,128)} fusion(f32[256,2048]{1,0:T(8,128)} %param.12, s32[64]{0:T(128)S(1)} %get-tuple-element.23, s32[64]{0:T(128)S(1)} %get-tuple-element.22, s32[2048]{0:T(1024)S(1)} %iota_add_fusion), kind=kOutput, calls=%fused_computation.10 | convolution fusion | flops 403308544 | bytes 2171392 | tf_op jit(solution)/shard_map/dot_general | solution.py:46
  15.9 1.7 fusion.25
  17.7 0.8 gather_fusion.2
  18.5 0.8 gather_fusion.3
  19.3 0.2 convolution_bitcast_fusion.2
  19.5 0.1 fusion.30
  19.6 60.6 %all-gather.5.cloned.1.call-done = f32[8192,64]{0,1:T(8,128)} async-done(((f32[256,64]{0,1:T(8,128)}), f32[8192,64]{0,1:T(8,128)}) %all-gather.5.cloned.1.call-update) | async-done | bytes 2097168 | tf_op jit(solution)/shard_map/all_gather | solution.py:9
  80.2 2.2 copy.15
  82.4 0.2 bitcast_reduce_fusion.1
  82.7 0.2 fusion.27
  82.9 57.1 %all-reduce.1 = (f32[64,64]{1,0:T(8,128)S(1)}, f32[64]{0:T(128)S(1)}) all-reduce(f32[64,64]{1,0:T(8,128)S(1)} %fusion.27, f32[64]{0:T(128)S(1)} %convolution_bitcast_fusion.2), channel_id=1, replica_groups=mesh['line'=16,'bus'=32] {'line'}, use_global_device_ids=true, to_apply=%region_1.3 | all-reduce | flops 4160 | bytes 33280 | tf_op jit(solution)/shard_map/psum | solution.py:48
  140.0 0.2 fusion.60
  140.2 0.2 fusion.59
  140.4 0.1 copy.13
  140.5 5.8 %cholesky.44 = f32[64,64]{1,0:T(8,128)S(1)} custom-call(f32[64,64]{1,0:T(8,128)S(1)} %fusion.46), custom_call_target="Cholesky" | custom-call | tf_op jit(solution)/shard_map/jit(cholesky)/cholesky | solution.py:57
  146.3 0.6 compare_reduce_fusion.1
  147.0 0.7 fusion.35
  147.6 4.9 %custom-call.11 = f32[1,64,64]{1,2,0:T(8,128)S(1)} custom-call(f32[1,64,64]{2,1,0:T(8,128)S(1)} %fusion.35), custom_call_target="InvertDiagBlocksLowerTriangular" | custom-call | tf_op jit(solution)/shard_map/triangular_solve/custom-call.2 | solution.py:18
  152.5 0.3 fusion.42
  152.8 0.2 fusion.44
  153.0 0.1 fusion.33
  153.2 7.4 %all-reduce.5.cloned.1.call-done = f32[64,2048]{1,0:T(8,128)} async-done(((f32[64,2048]{1,0:T(8,128)}), f32[64,2048]{1,0:T(8,128)}) %all-reduce.5.cloned.1.call-update) | async-done | bytes 524304 | tf_op jit(solution)/shard_map/psum | solution.py:49
  160.6 3.7 %fusion.1 = f32[256,2048]{1,0:T(8,128)S(1)} fusion(f32[256,2048]{1,0:T(8,128)} %param.12, f32[64,256]{1,0:T(8,128)S(1)} %fusion.44, f32[64,2048]{1,0:T(8,128)} %all-reduce.5.cloned.1.call-done, f32[256]{0:T(256)S(1)} %get-tuple-element.15), kind=kOutput, calls=%fused_computation.7 | convolution fusion | flops 403701760 | bytes 4785152 | tf_op jit(solution)/shard_map/dot_general | solution.py:61
  164.3 2.9 fusion.2
  167.2 0.2 all-reduce.7.cloned.1.call-start
  167.5 0.2 convolution_bitcast_fusion.1
  167.7 1.8 fusion.20
  169.5 54.5 %all-gather.7.cloned.1.call-done = f32[8192,64]{0,1:T(8,128)} async-done(((f32[256,64]{0,1:T(8,128)}), f32[8192,64]{0,1:T(8,128)}) %all-gather.7.cloned.1.call-update) | async-done | bytes 2097168 | tf_op jit(solution)/shard_map/all_gather | solution.py:9
  224.0 2.2 copy.16
  226.2 0.2 bitcast_reduce_fusion
  226.5 0.2 fusion.22
  226.7 57.0 %all-reduce = (f32[64,64]{1,0:T(8,128)S(1)}, f32[64]{0:T(128)S(1)}) all-reduce(f32[64,64]{1,0:T(8,128)S(1)} %fusion.22, f32[64]{0:T(128)S(1)} %convolution_bitcast_fusion.1), channel_id=1, replica_groups=mesh['line'=16,'bus'=32] {'line'}, use_global_device_ids=true, to_apply=%region_7.12 | all-reduce | flops 4160 | bytes 33280 | tf_op jit(solution)/shard_map/psum | solution.py:48
  283.7 0.2 fusion.62
  283.9 0.2 fusion.61
  284.1 0.1 copy.14
  284.2 5.8 %cholesky.55 = f32[64,64]{1,0:T(8,128)S(1)} custom-call(f32[64,64]{1,0:T(8,128)S(1)} %fusion.41), custom_call_target="Cholesky" | custom-call | tf_op jit(solution)/shard_map/jit(cholesky)/cholesky | solution.py:57
  290.1 0.6 compare_reduce_fusion
  290.7 0.7 fusion.36
  291.4 4.9 %custom-call.13 = f32[1,64,64]{1,2,0:T(8,128)S(1)} custom-call(f32[1,64,64]{2,1,0:T(8,128)S(1)} %fusion.36), custom_call_target="InvertDiagBlocksLowerTriangular" | custom-call | tf_op jit(solution)/shard_map/triangular_solve/custom-call.2 | solution.py:18
  296.3 0.3 fusion.37
  296.6 0.2 fusion.39
  296.8 0.1 fusion.31
  296.9 0.6 add_multiply_fusion
  297.5 7.1 %all-reduce.7.cloned.1.call-done = f32[64,2048]{1,0:T(8,128)} async-done(((f32[64,2048]{1,0:T(8,128)}), f32[64,2048]{1,0:T(8,128)}) %all-reduce.7.cloned.1.call-update) | async-done | bytes 524304 | tf_op jit(solution)/shard_map/psum | solution.py:49
  304.6 4.3 %fusion = f32[256,2048]{1,0:T(8,128)} fusion(f32[256,2048]{1,0:T(8,128)S(1)} %fusion.1, f32[64,256]{1,0:T(8,128)S(1)} %fusion.39, f32[64,2048]{1,0:T(8,128)} %all-reduce.7.cloned.1.call-done, f32[256]{0:T(256)S(1)} %get-tuple-element.13), kind=kOutput, calls=%fused_computation.5 | convolution fusion | flops 403701760 | bytes 4785152 | tf_op jit(solution)/shard_map/dot_general | solution.py:61
  (28 shorter events, 0.3 us)
Async XLA Ops:
  8.0 0.9 copy-start
  8.0 7.9 %copy-start.3 = (s32[2,64]{1,0:T(2,128)S(1)}, s32[2,64]{1,0:T(2,128)}, u32[]{:S(2)}) copy-start(s32[2,64]{1,0:T(2,128)} %param.16) | copy-start | bytes 1540
  8.0 7.9 %copy-start.2 = (f32[256,2048]{1,0:T(8,128)S(1)}, f32[256,2048]{1,0:T(8,128)}, u32[]{:S(2)}) copy-start(f32[256,2048]{1,0:T(8,128)} %param.12) | copy-start | bytes 6291460
  8.0 72.2 %all-gather.5.cloned.1.call-start = ((), (), s32[]{:S(2)}) async-start(), calls=%async_computation.2 | async-start | bytes 2162688 | tf_op jit(solution)/shard_map/all_gather | solution.py:9
  15.8 2.7 copy-start.1
  15.8 144.8 %all-reduce.5.cloned.1.call-start = ((), (), s32[]{:S(2)}) async-start(), calls=%async_computation | async-start | bytes 1048576 | tf_op jit(solution)/shard_map/psum | solution.py:49
  15.9 3.4 %copy-start.4 = (f32[256]{0:T(256)S(1)}, f32[256]{0:T(256)}, u32[]{:S(2)}) copy-start(f32[256]{0:T(256)} %param.13) | copy-start | bytes 3076
  17.7 206.3 %all-gather.7.cloned.1.call-start = ((), (), s32[]{:S(2)}) async-start(), calls=%async_computation.3 | async-start | bytes 2162688 | tf_op jit(solution)/shard_map/all_gather | solution.py:9
  167.2 137.4 %all-reduce.7.cloned.1.call-start = ((), (), s32[]{:S(2)}) async-start(), calls=%async_computation.1 | async-start | bytes 1048576 | tf_op jit(solution)/shard_map/psum | solution.py:49
Sparse Core Ops, SparseCore 0:
  15.9 64.2 all-gather.4
  167.4 56.5 all-gather.6
Sparse Core Ops, SparseCore 1:
  19.2 141.4 all-reduce.4
  170.7 133.8 all-reduce.6
